TPU v7x, 32 devices: a whole 2x2x4 slice. The times are simulated.
32 devices in a mesh: quad: 2 (over x), py: 4 (over y, core), pz: 4 (over z).
Axes of the slice: x: 2, y: 2, z: 4, core: 2. Of those that a mesh axis runs over, the one named last changes fastest.
Arguments:
- source_real: float32 [4, 16, 64, 512], P(None, None, 'py', 'pz'), may hold values from -6 to 6
- source_imag: float32 [4, 16, 64, 512], P(None, None, 'py', 'pz'), may hold values from -2 to 2
- potential: float32 [16, 64, 512], P(None, 'py', 'pz'), may hold values from 0 to 2
- center: float32 [1], replicated, may hold values from 4.5 to 6
- radius: float32 [1], replicated, may hold values from 1 to 2
Outputs:
- moments: float32 [4, 2, 4, 16, 64, 512], P(None, None, None, 'quad', 'py', 'pz')
All inputs are finite; a program needn't handle non-finite values.
Results may differ from a plain program's by a relative error of at most 0.0003.
Values sent between devices are 32-bit elements; how exact they have to be, the bound alone decides.
No kernel may reach another device: no remote copies, remote signals or barrier semaphores. Data moves between devices by JAX's collectives and lax.ppermute only.
A program may use at most 256 MiB of HBM per device.

v0:
```python
import math
import jax
import jax.numpy as jnp
from jax import lax
from jax.sharding import PartitionSpec as P

QPTS = 8
MOMS = 4
stencil_weights = (-205.0 / 72.0, 8.0 / 5.0, -1.0 / 5.0, 8.0 / 315.0, -1.0 / 560.0)


def padded_2(block, sides, width):
    for axis, dim in sides:
        count = lax.axis_size(axis)
        forward = [(i, i + 1) for i in range(count - 1)]
        forward.append((count - 1, 0))
        backward = [(target, source) for source, target in forward]
        low = lax.ppermute(
            lax.slice_in_dim(block, block.shape[dim] - width, None, axis=dim), axis, forward
        )
        high = lax.ppermute(lax.slice_in_dim(block, 0, width, axis=dim), axis, backward)
        block = jnp.concatenate([low, block, high], axis=dim)
    return block


def apply_operator(field, potential):
    padded = padded_2(field, (("py", 4), ("pz", 5)), 4)
    width_y = field.shape[4]
    width_z = field.shape[5]
    laplace = 3.0 * stencil_weights[0] * field
    for offset in range(1, 5):
        beside_all = jnp.roll(field, offset, 3) + jnp.roll(field, -offset, 3)
        beside_all = (
            beside_all + padded[:, :, :, :, 4 + offset : 4 + offset + width_y, 4 : 4 + width_z]
        )
        beside_all = (
            beside_all + padded[:, :, :, :, 4 - offset : 4 - offset + width_y, 4 : 4 + width_z]
        )
        beside_all = (
            beside_all + padded[:, :, :, :, 4 : 4 + width_y, 4 + offset : 4 + offset + width_z]
        )
        beside_all = (
            beside_all + padded[:, :, :, :, 4 : 4 + width_y, 4 - offset : 4 - offset + width_z]
        )
        laplace = laplace + stencil_weights[offset] * beside_all
    return -0.5 * laplace + potential * field


def complex_mul(left, right):
    return (left[0] * right[0] - left[1] * right[1], left[0] * right[1] + left[1] * right[0])


def complex_div(left, right):
    norm_sq = right[0] * right[0] + right[1] * right[1]
    return (
        (left[0] * right[0] + left[1] * right[1]) / norm_sq,
        (left[1] * right[0] - left[0] * right[1]) / norm_sq,
    )


def local_bilinear(left, right):
    both = complex_mul(left, right)
    return (jnp.sum(both[0], axis=(-3, -2, -1)), jnp.sum(both[1], axis=(-3, -2, -1)))


def spread(value):
    return (value[0][..., None, None, None], value[1][..., None, None, None])


def moment_terms(solution, angles, radius_value):
    orders = jnp.arange(1, MOMS + 1).astype(jnp.float32)
    phase = orders[:, None] * angles[None, :]
    weight_re = radius_value / QPTS * jnp.cos(phase)
    weight_im = radius_value / QPTS * jnp.sin(phase)
    highest = lax.Precision.HIGHEST
    real_part = jnp.einsum("kq,qsxyz->ksxyz", weight_re, solution[:, 0], precision=highest)
    real_part = real_part - jnp.einsum(
        "kq,qsxyz->ksxyz", weight_im, solution[:, 1], precision=highest
    )
    imag_part = jnp.einsum("kq,qsxyz->ksxyz", weight_re, solution[:, 1], precision=highest)
    imag_part = imag_part + jnp.einsum(
        "kq,qsxyz->ksxyz", weight_im, solution[:, 0], precision=highest
    )
    return jnp.stack([real_part, imag_part], 1)


def per_device(source_real, source_imag, potential, center, radius):
    groups = lax.axis_size("quad")
    local_count = QPTS // groups
    first_point = lax.axis_index("quad") * local_count
    indices = (first_point + jnp.arange(local_count)).astype(jnp.float32)
    angles = 2.0 * math.pi * (indices + 0.5) / QPTS
    shift_re = center[0] + radius[0] * jnp.cos(angles)
    shift_im = radius[0] * jnp.sin(angles)
    shift_pair = (shift_re[:, None], shift_im[:, None])
    shift_field = (shift_re[:, None, None, None, None], shift_im[:, None, None, None, None])
    source = (source_real, source_imag)
    applied = apply_operator(jnp.stack(source)[None], potential)[0]
    hsource = (applied[0], applied[1])
    rho_local = local_bilinear(source, source)
    curv_local = local_bilinear(source, hsource)
    totals = lax.psum((rho_local[0], rho_local[1], curv_local[0], curv_local[1]), ("py", "pz"))
    rho_first = (totals[0], totals[1])
    curv_first = (totals[2], totals[3])
    scaled = complex_mul(shift_pair, rho_first)
    denom = (scaled[0] - curv_first[0], scaled[1] - curv_first[1])
    alpha_first = complex_div(rho_first, denom)
    alpha_wide = spread(alpha_first)
    first_iterate = complex_mul(alpha_wide, source)
    shifted = complex_mul(shift_field, source)
    image = (shifted[0] - hsource[0], shifted[1] - hsource[1])
    moved = complex_mul(alpha_wide, image)
    residual = (source[0] - moved[0], source[1] - moved[1])
    hres = apply_operator(jnp.stack(residual, 1), potential)
    shifted_res = complex_mul(shift_field, residual)
    image_res = (shifted_res[0] - hres[:, 0], shifted_res[1] - hres[:, 1])
    rho_part = local_bilinear(residual, residual)
    mixed_part = local_bilinear(residual, image_res)
    paired = lax.psum((rho_part[0], rho_part[1], mixed_part[0], mixed_part[1]), ("py", "pz"))
    rho_next = (paired[0], paired[1])
    mixed = (paired[2], paired[3])
    beta = complex_div(rho_next, rho_first)
    carried = complex_mul(spread(beta), source)
    direction = (residual[0] + carried[0], residual[1] + carried[1])
    correction = complex_div(complex_mul(beta, rho_next), alpha_first)
    curv_next = (mixed[0] - correction[0], mixed[1] - correction[1])
    alpha_next = complex_div(rho_next, curv_next)
    step_part = complex_mul(spread(alpha_next), direction)
    solution = jnp.stack((first_iterate[0] + step_part[0], first_iterate[1] + step_part[1]), 1)
    terms = moment_terms(solution, angles, radius[0])
    return lax.psum_scatter(terms, "quad", scatter_dimension=3, tiled=True)


def solution(mesh):
    in_specs = (P(None, None, "py", "pz"), P(None, None, "py", "pz"), P(None, "py", "pz"), P(), P())
    out_specs = P(None, None, None, "quad", "py", "pz")
    return jax.shard_map(
        per_device, mesh=mesh, in_specs=in_specs, out_specs=out_specs, check_vma=False
    )
```

profile of v0, /device:TPU:0, one launch (start us, length us, event | category | flops | bytes accessed | tf_op | source)
XLA Modules:
  0.0 492.0 jit_solution(7060185690487794828)
XLA Ops:
  9.0 2.4 collective-permute-start
  12.9 1.6 fusion.122
  21.1 2.6 copy.87
  23.7 2.6 copy.88
  38.7 2.2 fusion.117
  41.0 3.0 copy.95
  44.0 1.6 collective-permute-start.3
  45.5 3.0 copy.92
  48.5 2.8 collective-permute-start.2
  51.3 4.5 fusion.50
  55.8 1.7 copy.93
  57.5 3.0 copy.96
  60.7 2.9 copy.94
  63.6 17.7 %fusion.58 = f32[1,2,4,16,16,128]{5,4,3,2,1,0:T(8,128)S(1)} fusion(f32[1,2,4,16,24,4]{5,4,3,2,1,0:T(8,128)} %copy.96, f32[1,2,4,16,24,128]{5,4,3,2,1,0:T(8,128)} %copy.93, f32[1,2,4,16,24,4]{5,4,3,2,1,0:T(8,128)} %copy.94, f32[1,2,4,15,16,128]{5,4,3,2,1,0:T(8,128)} %copy.87, f32[1,2,4,1,16,128]{5,4,3,2,1,0:T(8,128)} %bitcast.76, ...), kind=kLoop, calls=%fused_computation.166 | loop fusion | flops 12845056 | bytes 20676608 | tf_op jit(solution)/shard_map/add | solution.py:46
  82.9 34.7 %all-reduce.1 = (f32[4]{0:T(128)S(1)}, f32[4]{0:T(128)S(1)}, f32[4]{0:T(128)S(1)}, f32[4]{0:T(128)S(1)}) all-reduce(f32[4]{0:T(128)S(1)} %get-tuple-element.10, f32[4]{0:T(128)S(1)} %get-tuple-element.9, f32[4]{0:T(128)S(1)} %get-tuple-element.12, f32[4]{0:T(128)S(1)} %get-tuple-element.11), channel_id=1, replica_groups=mesh['quad'=2,'py'=4,'pz'=4] {'py','pz'}, use_global_device_ids=true, to_apply=%region_7.8 | all-reduce | flops 16 | bytes 128 | tf_op jit(solution)/shard_map/psum | solution.py:102
  117.7 2.4 add_subtract_fusion
  120.8 2.5 pad_maximum_fusion.1
  124.4 3.5 fusion.31
  127.8 1.6 fusion.76
  133.6 19.1 %copy.121 = f32[4,2,4,16,16,128]{4,3,5,2,1,0:T(8,128)} copy(f32[4,2,4,16,16,128]{5,4,3,2,1,0:T(8,128)} %pad_maximum_fusion.1) | data formatting | bytes 8388608 | tf_op jit(solution)/shard_map/stack | solution.py:114
  152.7 2.6 fusion.89
  155.3 3.4 fusion.29
  158.7 3.2 fusion.27
  161.9 3.4 fusion.25
  165.4 18.9 %copy.122 = f32[4,2,4,16,4,128]{4,3,5,2,1,0:T(8,128)} copy(f32[4,2,4,16,4,128]{5,3,4,2,1,0:T(8,128)} %collective-permute-done.4) | data formatting | bytes 2097152 | tf_op jit(solution)/shard_map/ppermute | solution.py:21
  184.3 18.6 %copy.120 = f32[4,2,4,16,4,128]{4,3,5,2,1,0:T(8,128)} copy(f32[4,2,4,16,4,128]{5,3,4,2,1,0:T(8,128)} %collective-permute-done.5) | data formatting | bytes 2097152 | tf_op jit(solution)/shard_map/ppermute | solution.py:18
  202.9 43.9 %pad_maximum_fusion = f32[4,2,4,16,24,128]{4,3,5,2,1,0:T(8,128)} fusion(f32[4,2,4,16,4,128]{4,3,5,2,1,0:T(8,128)} %copy.122, f32[4,2,4,16,16,128]{4,3,5,2,1,0:T(8,128)} %copy.121, f32[4,2,4,16,4,128]{4,3,5,2,1,0:T(8,128)} %copy.120), kind=kLoop, calls=%fused_computation | loop fusion | flops 3145728 | bytes 12582912 | tf_op jit(solution)/shard_map/concatenate | solution.py:22
  246.8 3.1 fusion.116
  249.9 4.0 collective-permute-start.6
  253.9 1.6 copy.117
  255.6 1.6 copy.119
  257.3 5.5 %pad_maximum_fusion.2 = (f32[4,2,4,16,20,128]{5,4,3,2,1,0:T(8,128)}, f32[4,2,4,16,20,128]{5,4,3,2,1,0:T(8,128)}) fusion(f32[4,2,4,16,4,128]{5,4,3,2,1,0:T(4,128)S(1)} %copy.117, f32[4,1,4,16,16,128]{5,4,3,2,1,0:T(8,128)S(1)} %get-tuple-element.48, f32[4,1,4,16,16,128]{5,4,3,2,1,0:T(8,128)S(1)} %copy-done.2, f32[4,2,4,16,4,128]{5,4,3,2,1,0:T(4,128)S(1)} %copy.119), kind=kLoop, calls=%fused_computation.50 | loop fusion | flops 5242880 | bytes 16777216 | tf_op jit(solution)/shard_map/concatenate | solution.py:22
  262.7 22.1 %copy.123 = f32[4,2,4,16,24,128]{5,4,3,2,1,0:T(8,128)} copy(f32[4,2,4,16,24,128]{4,3,5,2,1,0:T(8,128)} %pad_maximum_fusion) | data formatting | bytes 12582912 | tf_op jit(solution)/shard_map/concatenate | solution.py:22
  284.8 6.1 %copy.125 = f32[4,2,4,16,24,4]{5,4,3,2,1,0:T(8,128)} copy(f32[4,2,4,16,24,4]{4,3,5,2,1,0:T(8,128)} %collective-permute-done.7) | data formatting | bytes 393216 | tf_op jit(solution)/shard_map/ppermute | solution.py:18
  291.0 7.0 %collective-permute-done.6 = f32[4,2,4,16,24,4]{4,3,5,2,1,0:T(8,128)} collective-permute-done((f32[4,2,4,16,24,4]{4,3,5,2,1,0:T(8,128)}, f32[4,2,4,16,24,4]{4,3,5,2,1,0:T(8,128)}, u32[]{:S(2)}, u32[]{:S(2)}) %collective-permute-start.6) | collective-permute-done | bytes 196640 | tf_op jit(solution)/shard_map/ppermute | solution.py:21
  298.0 6.0 %copy.124 = f32[4,2,4,16,24,4]{5,4,3,2,1,0:T(8,128)} copy(f32[4,2,4,16,24,4]{4,3,5,2,1,0:T(8,128)} %collective-permute-done.6) | data formatting | bytes 393216 | tf_op jit(solution)/shard_map/ppermute | solution.py:21
  304.0 62.2 %fusion.6 = f32[4,2,4,16,16,128]{5,4,3,2,1,0:T(8,128)} fusion(f32[4,2,4,16,24,4]{5,4,3,2,1,0:T(8,128)} %copy.125, f32[4,2,4,16,24,128]{5,4,3,2,1,0:T(8,128)} %copy.123, f32[4,2,4,16,24,4]{5,4,3,2,1,0:T(8,128)} %copy.124, f32[4,2,4,16,20,128]{5,4,3,2,1,0:T(8,128)} %get-tuple-element.43, f32[4,2,4,16,20,128]{5,4,3,2,1,0:T(8,128)} %get-tuple-element.42, ...), kind=kLoop, calls=%fused_computation.70 | loop fusion | flops 51380224 | bytes 82313216 | tf_op jit(solution)/shard_map/add | solution.py:46
  366.3 5.0 %subtract_reduce_fusion = (f32[4,4]{1,0:T(4,128)S(1)}, f32[4,4]{1,0:T(4,128)S(1)}, f32[4,4]{1,0:T(4,128)S(1)}, f32[4,4]{1,0:T(4,128)S(1)}) fusion(f32[4,2,4,16,16,128]{5,4,3,2,1,0:T(8,128)} %fusion.6, f32[4]{0:T(128)S(1)} %get-tuple-element.88, f32[4]{0:T(128)S(1)} %get-tuple-element.89, f32[4,16,16,128]{3,2,1,0:T(8,128)S(1)} %copy-done.8, ...), kind=kLoop, calls=%fused_computation.129 | loop fusion | flops 20447168 | bytes 6291872 | tf_op jit(solution)/shard_map/reduce_sum | solution.py:63
  371.3 30.6 %all-reduce = (f32[4,4]{1,0:T(4,128)S(1)}, f32[4,4]{1,0:T(4,128)S(1)}, f32[4,4]{1,0:T(4,128)S(1)}, f32[4,4]{1,0:T(4,128)S(1)}) all-reduce(f32[4,4]{1,0:T(4,128)S(1)} %get-tuple-element.8, f32[4,4]{1,0:T(4,128)S(1)} %get-tuple-element.6, f32[4,4]{1,0:T(4,128)S(1)} %get-tuple-element.7, ...), channel_id=1, replica_groups=mesh['quad'=2,'py'=4,'pz'=4] {'py','pz'}, use_global_device_ids=true, to_apply=%region_9.10 | all-reduce | flops 64 | bytes 512 | tf_op jit(solution)/shard_map/psum | solution.py:119
  402.2 2.9 subtract_add_fusion
  405.1 4.4 fusion.34
  409.5 4.4 fusion.36
  413.9 4.6 add_bitcast_fusion
  418.5 4.9 %subtract_bitcast_fusion = f32[4,1,4,16,16,128]{5,0,4,3,2,1:T(4,128)S(1)} fusion(f32[4,4,16,16,128]{4,0,3,2,1:T(4,128)S(1)} %fusion.36, f32[4,4,16,16,128]{4,3,2,1,0:T(8,128)S(1)} %get-tuple-element.46, f32[4]{0:T(128)S(1)} %copy-done.20, f32[4]{0:T(128)S(1)} %copy-done.21, f32[]{:T(128)S(6)} %div.49), kind=kOutput, calls=%fused_computation.123 | convolution fusion | flops 25690144 | bytes 6291492 | tf_op jit(solution)/shard_map/kq,qsxyz->ksxyz/dot_general | solution.py:76
  423.4 2.0 pad_maximum_fusion.5
  425.5 2.6 copy.132
  428.1 53.6 %reduce-scatter.2.cloned.1.call-done = f32[4,2,4,8,16,128]{5,4,2,1,0,3:T(8,128)} async-done(((f32[4,2,4,16,16,128]{5,4,2,1,0,3:T(8,128)}), f32[4,2,4,8,16,128]{5,4,2,1,0,3:T(8,128)}) %reduce-scatter.2.cloned.1.call-update) | async-done | bytes 2097168 | tf_op jit(solution)/shard_map/reduce_scatter | solution.py:131
  481.6 3.2 copy.133
  (112 shorter events, 29.5 us)
Async XLA Ops:
  6.5 475.1 %reduce-scatter.2.cloned.1.call-start = ((), (), s32[]{:S(2)}) async-start(), calls=%async_computation.1 | async-start | bytes 6291456 | tf_op jit(solution)/shard_map/reduce_scatter | solution.py:131
  9.0 28.6 %collective-permute-start = (f32[1,2,4,16,4,128]{5,3,4,2,1,0:T(8,128)}, f32[1,2,4,16,4,128]{5,3,4,2,1,0:T(8,128)}, u32[]{:S(2)}, u32[]{:S(2)}) collective-permute-start(f32[1,2,4,16,4,128]{5,3,4,2,1,0:T(8,128)} %get-tuple-element.83), channel_id=1, source_target_pairs={{4,0},{8,4},{12,8},{0,12},{5,1},{9,5},{13,9},{1,13},{6,2},{10,6},{... | collective-permute-start | bytes 786440 | tf_op jit(solution)/shard_map/ppermute | solution.py:21
  11.4 26.2 %collective-permute-start.1 = (f32[1,2,4,16,4,128]{5,3,4,2,1,0:T(8,128)}, f32[1,2,4,16,4,128]{5,3,4,2,1,0:T(8,128)}, u32[]{:S(2)}, u32[]{:S(2)}) collective-permute-start(f32[1,2,4,16,4,128]{5,3,4,2,1,0:T(8,128)} %get-tuple-element.82), channel_id=1, source_target_pairs={{0,4},{4,8},{8,12},{12,0},{1,5},{5,9},{9,13},{13,1},{2,6},{6,10},{... | collective-permute-start | bytes 786440 | tf_op jit(solution)/shard_map/ppermute | solution.py:18
  20.0 6.3 %copy-start.14 = (f32[1,2,4,14,16,128]{5,3,4,2,1,0:T(8,128)S(1)}, f32[1,2,4,14,16,128]{5,3,4,2,1,0:T(8,128)}, u32[]{:S(2)}) copy-start(f32[1,2,4,14,16,128]{5,3,4,2,1,0:T(8,128)} %get-tuple-element.75) | copy-start | bytes 2752516
  20.0 7.5 %copy-start.19 = (f32[1,2,4,2,16,128]{5,3,4,2,1,0:T(2,128)S(1)}, f32[1,2,4,2,16,128]{5,3,4,2,1,0:T(2,128)}, u32[]{:S(2)}) copy-start(f32[1,2,4,2,16,128]{5,3,4,2,1,0:T(2,128)} %get-tuple-element.77) | copy-start | bytes 393220
  21.1 7.7 %copy-start.13 = (f32[1,2,4,14,16,128]{5,3,4,2,1,0:T(8,128)S(1)}, f32[1,2,4,14,16,128]{5,3,4,2,1,0:T(8,128)}, u32[]{:S(2)}) copy-start(f32[1,2,4,14,16,128]{5,3,4,2,1,0:T(8,128)} %get-tuple-element.74) | copy-start | bytes 2752516
  23.7 6.3 %copy-start.12 = (f32[1,2,4,13,16,128]{5,3,4,2,1,0:T(8,128)S(1)}, f32[1,2,4,13,16,128]{5,3,4,2,1,0:T(8,128)}, u32[]{:S(2)}) copy-start(f32[1,2,4,13,16,128]{5,3,4,2,1,0:T(8,128)} %get-tuple-element.71) | copy-start | bytes 2555908
  26.3 5.0 %copy-start.15 = (f32[1,2,4,3,16,128]{5,3,4,2,1,0:T(4,128)S(1)}, f32[1,2,4,3,16,128]{5,3,4,2,1,0:T(4,128)}, u32[]{:S(2)}) copy-start(f32[1,2,4,3,16,128]{5,3,4,2,1,0:T(4,128)} %get-tuple-element.73) | copy-start | bytes 589828
  27.5 5.1 %copy-start.11 = (f32[1,2,4,13,16,128]{5,3,4,2,1,0:T(8,128)S(1)}, f32[1,2,4,13,16,128]{5,3,4,2,1,0:T(8,128)}, u32[]{:S(2)}) copy-start(f32[1,2,4,13,16,128]{5,3,4,2,1,0:T(8,128)} %get-tuple-element.70) | copy-start | bytes 2555908
  30.1 4.9 copy-start.17
  30.1 4.9 copy-start.16
  44.0 13.5 %collective-permute-start.3 = (f32[1,2,4,16,24,4]{4,3,5,2,1,0:T(8,128)}, f32[1,2,4,16,24,4]{4,3,5,2,1,0:T(8,128)}, u32[]{:S(2)}, u32[]{:S(2)}) collective-permute-start(f32[1,2,4,16,24,4]{4,3,5,2,1,0:T(8,128)} %copy.95), channel_id=1, source_target_pairs={{0,1},{1,2},{2,3},{3,0},{4,5},{5,6},{6,7},{7,4},{8,9},{9,10},{10,1... | collective-permute-start | bytes 147464 | tf_op jit(solution)/shard_map/ppermute | solution.py:18
  48.5 12.1 %collective-permute-start.2 = (f32[1,2,4,16,24,4]{4,3,5,2,1,0:T(8,128)}, f32[1,2,4,16,24,4]{4,3,5,2,1,0:T(8,128)}, u32[]{:S(2)}, u32[]{:S(2)}) collective-permute-start(f32[1,2,4,16,24,4]{4,3,5,2,1,0:T(8,128)} %copy.92), channel_id=1, source_target_pairs={{1,0},{2,1},{3,2},{0,3},{5,4},{6,5},{7,6},{4,7},{9,8},{10,9},{11,1... | collective-permute-start | bytes 147464 | tf_op jit(solution)/shard_map/ppermute | solution.py:21
  55.8 7.8 %copy-start.3 = (f32[4,16,16,128]{3,2,1,0:T(8,128)S(1)}, f32[4,16,16,128]{3,2,1,0:T(8,128)}, u32[]{:S(2)}) copy-start(f32[4,16,16,128]{3,2,1,0:T(8,128)} %param.6) | copy-start | bytes 1572868
  55.8 7.8 %copy-start.4 = (f32[4,16,16,128]{3,2,1,0:T(8,128)S(1)}, f32[4,16,16,128]{3,2,1,0:T(8,128)}, u32[]{:S(2)}) copy-start(f32[4,16,16,128]{3,2,1,0:T(8,128)} %param.5) | copy-start | bytes 1572868
  55.8 7.8 %copy-start.18 = (f32[16,16,128]{2,1,0:T(8,128)S(1)}, f32[16,16,128]{2,1,0:T(8,128)}, u32[]{:S(2)}) copy-start(f32[16,16,128]{2,1,0:T(8,128)} %param.7) | copy-start | bytes 393220
  57.5 6.1 %copy-start.10 = (f32[1,2,4,16,16,128]{5,3,4,2,1,0:T(8,128)S(1)}, f32[1,2,4,16,16,128]{5,3,4,2,1,0:T(8,128)}, u32[]{:S(2)}) copy-start(f32[1,2,4,16,16,128]{5,3,4,2,1,0:T(8,128)} %get-tuple-element.52) | copy-start | bytes 3145732
  81.3 36.4 %copy-start.5 = (f32[4,16,16,128]{3,2,1,0:T(8,128)S(1)}, f32[4,16,16,128]{3,2,1,0:T(8,128)}, u32[]{:S(2)}) copy-start(f32[4,16,16,128]{3,2,1,0:T(8,128)} %param.5) | copy-start | bytes 1572868
  117.6 2.5 copy-start.22
  117.6 2.6 copy-start.24
  117.6 11.8 %copy-start.26 = (f32[4]{0:T(128)}, f32[4]{0:T(128)S(1)}, u32[]{:S(2)}) copy-start(f32[4]{0:T(128)S(1)} %get-tuple-element.19) | copy-start | bytes 52
  117.6 11.8 %copy-start.28 = (f32[4]{0:T(128)}, f32[4]{0:T(128)S(1)}, u32[]{:S(2)}) copy-start(f32[4]{0:T(128)S(1)} %get-tuple-element.20) | copy-start | bytes 52
  120.2 12.7 %copy-start = (f32[4,1,4,16,16,128]{5,4,3,2,1,0:T(8,128)}, f32[4,1,4,16,16,128]{5,4,3,2,1,0:T(8,128)S(1)}, u32[]{:S(2)}) copy-start(f32[4,1,4,16,16,128]{5,4,3,2,1,0:T(8,128)S(1)} %get-tuple-element.49) | copy-start | bytes 6291460
  131.1 34.3 %collective-permute-start.4 = (f32[4,2,4,16,4,128]{5,3,4,2,1,0:T(8,128)}, f32[4,2,4,16,4,128]{5,3,4,2,1,0:T(8,128)}, u32[]{:S(2)}, u32[]{:S(2)}) collective-permute-start(f32[4,2,4,16,4,128]{5,3,4,2,1,0:T(8,128)} %copy.144), channel_id=1, source_target_pairs={{4,0},{8,4},{12,8},{0,12},{5,1},{9,5},{13,9},{1,13},{6,2},{10,6},{... | collective-permute-start | bytes 3145736 | tf_op jit(solution)/shard_map/ppermute | solution.py:21
  132.2 52.1 %collective-permute-start.5 = (f32[4,2,4,16,4,128]{5,3,4,2,1,0:T(8,128)}, f32[4,2,4,16,4,128]{5,3,4,2,1,0:T(8,128)}, u32[]{:S(2)}, u32[]{:S(2)}) collective-permute-start(f32[4,2,4,16,4,128]{5,3,4,2,1,0:T(8,128)} %copy.145), channel_id=1, source_target_pairs={{0,4},{4,8},{8,12},{12,0},{1,5},{5,9},{9,13},{13,1},{2,6},{6,10},{... | collective-permute-start | bytes 3145736 | tf_op jit(solution)/shard_map/ppermute | solution.py:18
  152.7 2.6 copy-start.1
  249.9 7.3 %copy-start.2 = (f32[4,1,4,16,16,128]{5,4,3,2,1,0:T(8,128)S(1)}, f32[4,1,4,16,16,128]{5,4,3,2,1,0:T(8,128)}, u32[]{:S(2)}) copy-start(f32[4,1,4,16,16,128]{5,4,3,2,1,0:T(8,128)} %copy-done) | copy-start | bytes 6291460
  249.9 34.9 %collective-permute-start.7 = (f32[4,2,4,16,24,4]{4,3,5,2,1,0:T(8,128)}, f32[4,2,4,16,24,4]{4,3,5,2,1,0:T(8,128)}, u32[]{:S(2)}, u32[]{:S(2)}) collective-permute-start(f32[4,2,4,16,24,4]{4,3,5,2,1,0:T(8,128)} %get-tuple-element.25), channel_id=1, source_target_pairs={{0,1},{1,2},{2,3},{3,0},{4,5},{5,6},{6,7},{7,4},{8,9},{9,10},{10,1... | collective-permute-start | bytes 589832 | tf_op jit(solution)/shard_map/ppermute | solution.py:18
  249.9 48.1 %collective-permute-start.6 = (f32[4,2,4,16,24,4]{4,3,5,2,1,0:T(8,128)}, f32[4,2,4,16,24,4]{4,3,5,2,1,0:T(8,128)}, u32[]{:S(2)}, u32[]{:S(2)}) collective-permute-start(f32[4,2,4,16,24,4]{4,3,5,2,1,0:T(8,128)} %get-tuple-element.24), channel_id=1, source_target_pairs={{1,0},{2,1},{3,2},{0,3},{5,4},{6,5},{7,6},{4,7},{9,8},{10,9},{11,1... | collective-permute-start | bytes 589832 | tf_op jit(solution)/shard_map/ppermute | solution.py:21
  304.0 62.2 %copy-start.6 = (f32[4,16,16,128]{3,2,1,0:T(8,128)S(1)}, f32[4,16,16,128]{3,2,1,0:T(8,128)}, u32[]{:S(2)}) copy-start(f32[4,16,16,128]{3,2,1,0:T(8,128)} %get-tuple-element.60) | copy-start | bytes 1572868
  304.0 62.2 %copy-start.8 = (f32[4,16,16,128]{3,2,1,0:T(8,128)S(1)}, f32[4,16,16,128]{3,2,1,0:T(8,128)}, u32[]{:S(2)}) copy-start(f32[4,16,16,128]{3,2,1,0:T(8,128)} %get-tuple-element.61) | copy-start | bytes 1572868
  366.3 35.7 %copy-start.23 = (f32[4]{0:T(128)S(1)}, f32[4]{0:T(128)}, u32[]{:S(2)}) copy-start(f32[4]{0:T(128)} %copy-done.22) | copy-start | bytes 52
  366.3 35.7 %copy-start.25 = (f32[4]{0:T(128)S(1)}, f32[4]{0:T(128)}, u32[]{:S(2)}) copy-start(f32[4]{0:T(128)} %copy-done.24) | copy-start | bytes 52
  366.3 35.7 %copy-start.27 = (f32[4]{0:T(128)S(1)}, f32[4]{0:T(128)}, u32[]{:S(2)}) copy-start(f32[4]{0:T(128)} %copy-done.26) | copy-start | bytes 52
  366.3 35.7 %copy-start.29 = (f32[4]{0:T(128)S(1)}, f32[4]{0:T(128)}, u32[]{:S(2)}) copy-start(f32[4]{0:T(128)} %copy-done.28) | copy-start | bytes 52
  366.3 35.7 %copy-start.30 = (f32[4]{0:T(128)S(1)}, f32[4]{0:T(128)}, u32[]{:S(2)}) copy-start(f32[4]{0:T(128)} %multiply_add_fusion.4) | copy-start | bytes 52
  366.3 35.8 %copy-start.7 = (f32[4,16,16,128]{3,2,1,0:T(8,128)S(1)}, f32[4,16,16,128]{3,2,1,0:T(8,128)}, u32[]{:S(2)}) copy-start(f32[4,16,16,128]{3,2,1,0:T(8,128)} %get-tuple-element.60) | copy-start | bytes 1572868
  366.3 35.8 %copy-start.9 = (f32[4,16,16,128]{3,2,1,0:T(8,128)S(1)}, f32[4,16,16,128]{3,2,1,0:T(8,128)}, u32[]{:S(2)}) copy-start(f32[4,16,16,128]{3,2,1,0:T(8,128)} %get-tuple-element.61) | copy-start | bytes 1572868
  402.2 2.9 copy-start.20
  402.2 2.9 copy-start.21
Sparse Core Ops, SparseCore 0:
  428.2 53.3 reduce-scatter.1
where the time goes:
time: 499 us; the launch traced here: 492 us
  other arithmetic  173 us (35%)
  local copies, waits for them, and re-layouts  147 us (29%)
  blocking collectives  65.3 us (13%)
  waiting for transfers between devices  60.8 us (12%)
  matrix products  18.3 us (4%)
  between operations  15.5 us (3%)
  starting transfers between devices  11.4 us (2%)
    add x2, other arithmetic, apply_operator(): return -0.5 * laplace + potential * field  79.9 us
    concatenate x4, other arithmetic, padded_2(): block = jnp.concatenate([low, block, high], axis=dim)  55 us
    reduce_scatter x1, waiting for transfers between devices, per_device(): return lax.psum_scatter(terms, 'quad', scatter_dimension=3, tiled=True)  53.6 us
    psum x1, blocking collectives, per_device(): lax.psum((rho_local[0], rho_local[1], curv_local[0], curv_local[1]), ('py...  34.7 us
    psum x1, blocking collectives, per_device(): lax.psum((rho_part[0], rho_part[1], mixed_part[0], mixed_part[1]), ('py',...  30.6 us
    ppermute x4, local copies, waits for them, and re-layouts, padded_2(): lax.ppermute(lax.slice_in_dim(block, 0, width, axis=dim), axis, backward)  29.5 us
    ppermute x4, local copies, waits for them, and re-layouts, padded_2(): lax.ppermute(lax.slice_in_dim(block, block.shape[dim] - width, None, axis...  29.4 us
    concatenate x2, local copies, waits for them, and re-layouts, padded_2(): block = jnp.concatenate([low, block, high], axis=dim)  23.7 us
  transfers between devices with their start and end apart: 9, of which 3 were waited for; matrix products, arithmetic and copies ran while one was open for 26% of the time, Pallas kernels for 0%

commit v1 on v0

--- a/solution.py
+++ b/solution.py
@@ -116,7 +116,8 @@
     image_res = (shifted_res[0] - hres[:, 0], shifted_res[1] - hres[:, 1])
     rho_part = local_bilinear(residual, residual)
     mixed_part = local_bilinear(residual, image_res)
-    paired = lax.psum((rho_part[0], rho_part[1], mixed_part[0], mixed_part[1]), ("py", "pz"))
+    trace_squares = lambda vals: lax.psum(lax.psum(vals, "pz"), "py")
+    paired = trace_squares((rho_part[0], rho_part[1], mixed_part[0], mixed_part[1]))
     rho_next = (paired[0], paired[1])
     mixed = (paired[2], paired[3])
     beta = complex_div(rho_next, rho_first)

time: 499 us -> 484 us (0.970)
  blocking collectives: 65.3 us -> 51.2 us
    psum x1 -> x2, blocking collectives: 30.6 us -> 16.5 us  [per_device(): trace_squares = lambda vals: lax.psum(lax.psum(vals, 'pz'), 'py')]
where the time goes in v1:
time: 484 us; the launch traced here: 477 us
  other arithmetic  174 us (36%)
  local copies, waits for them, and re-layouts  147 us (30%)
  waiting for transfers between devices  59.1 us (12%)
  blocking collectives  51.2 us (11%)
  matrix products  18.3 us (4%)
  between operations  15.5 us (3%)
  starting transfers between devices  11.4 us (2%)
    add x2, other arithmetic, apply_operator(): return -0.5 * laplace + potential * field  80.9 us
    concatenate x4, other arithmetic, padded_2(): block = jnp.concatenate([low, block, high], axis=dim)  54.9 us
    reduce_scatter x1, waiting for transfers between devices, per_device(): return lax.psum_scatter(terms, 'quad', scatter_dimension=3, tiled=True)  51.8 us
    psum x1, blocking collectives, per_device(): lax.psum((rho_local[0], rho_local[1], curv_local[0], curv_local[1]), ('py...  34.7 us
    ppermute x4, local copies, waits for them, and re-layouts, padded_2(): lax.ppermute(lax.slice_in_dim(block, 0, width, axis=dim), axis, backward)  29.5 us
    ppermute x4, local copies, waits for them, and re-layouts, padded_2(): lax.ppermute(lax.slice_in_dim(block, block.shape[dim] - width, None, axis...  29.4 us
    concatenate x2, local copies, waits for them, and re-layouts, padded_2(): block = jnp.concatenate([low, block, high], axis=dim)  23.7 us
    slice x22, local copies, waits for them, and re-layouts, apply_operator(): beside_all = jnp.roll(field, offset, 3) + jnp.roll(field, -offset, 3)  23.7 us
  transfers between devices with their start and end apart: 9, of which 3 were waited for; matrix products, arithmetic and copies ran while one was open for 26% of the time, Pallas kernels for 0%

profile of v1, /device:TPU:0, one launch (start us, length us, event | category | flops | bytes accessed | tf_op | source)
XLA Modules:
  0.0 477.0 jit_solution(3406231870584111403)
XLA Ops:
  9.0 2.4 collective-permute-start
  12.9 1.6 fusion.122
  21.1 2.6 copy.87
  23.7 2.6 copy.88
  38.7 2.2 fusion.117
  41.0 3.0 copy.95
  45.5 3.0 copy.92
  48.5 2.8 collective-permute-start.2
  51.3 4.5 fusion.50
  55.8 1.7 copy.93
  57.5 3.0 copy.96
  60.6 2.9 copy.94
  63.6 17.9 %fusion.58 = f32[1,2,4,16,16,128]{5,4,3,2,1,0:T(8,128)S(1)} fusion(f32[1,2,4,16,24,4]{5,4,3,2,1,0:T(8,128)} %copy.96, f32[1,2,4,16,24,128]{5,4,3,2,1,0:T(8,128)} %copy.93, f32[1,2,4,16,24,4]{5,4,3,2,1,0:T(8,128)} %copy.94, f32[1,2,4,15,16,128]{5,4,3,2,1,0:T(8,128)} %copy.87, f32[1,2,4,1,16,128]{5,4,3,2,1,0:T(8,128)} %bitcast.76, ...), kind=kLoop, calls=%fused_computation.166 | loop fusion | flops 12845056 | bytes 20676608 | tf_op jit(solution)/shard_map/add | solution.py:46
  83.0 34.7 %all-reduce = (f32[4]{0:T(128)S(1)}, f32[4]{0:T(128)S(1)}, f32[4]{0:T(128)S(1)}, f32[4]{0:T(128)S(1)}) all-reduce(f32[4]{0:T(128)S(1)} %get-tuple-element.10, f32[4]{0:T(128)S(1)} %get-tuple-element.9, f32[4]{0:T(128)S(1)} %get-tuple-element.12, f32[4]{0:T(128)S(1)} %get-tuple-element.11), channel_id=1, replica_groups=mesh['quad'=2,'py'=4,'pz'=4] {'py','pz'}, use_global_device_ids=true, to_apply=%region_7.8 | all-reduce | flops 16 | bytes 128 | tf_op jit(solution)/shard_map/psum | solution.py:102
  117.8 2.4 add_subtract_fusion
  120.9 2.4 pad_maximum_fusion.1
  124.4 3.5 fusion.31
  127.9 1.6 fusion.76
  133.7 19.1 %copy.121 = f32[4,2,4,16,16,128]{4,3,5,2,1,0:T(8,128)} copy(f32[4,2,4,16,16,128]{5,4,3,2,1,0:T(8,128)} %pad_maximum_fusion.1) | data formatting | bytes 8388608 | tf_op jit(solution)/shard_map/stack | solution.py:114
  152.8 2.6 fusion.89
  155.4 3.4 fusion.29
  158.8 3.2 fusion.27
  162.0 3.4 fusion.25
  165.5 18.9 %copy.122 = f32[4,2,4,16,4,128]{4,3,5,2,1,0:T(8,128)} copy(f32[4,2,4,16,4,128]{5,3,4,2,1,0:T(8,128)} %collective-permute-done.4) | data formatting | bytes 2097152 | tf_op jit(solution)/shard_map/ppermute | solution.py:21
  184.4 18.6 %copy.120 = f32[4,2,4,16,4,128]{4,3,5,2,1,0:T(8,128)} copy(f32[4,2,4,16,4,128]{5,3,4,2,1,0:T(8,128)} %collective-permute-done.5) | data formatting | bytes 2097152 | tf_op jit(solution)/shard_map/ppermute | solution.py:18
  202.9 43.9 %pad_maximum_fusion = f32[4,2,4,16,24,128]{4,3,5,2,1,0:T(8,128)} fusion(f32[4,2,4,16,4,128]{4,3,5,2,1,0:T(8,128)} %copy.122, f32[4,2,4,16,16,128]{4,3,5,2,1,0:T(8,128)} %copy.121, f32[4,2,4,16,4,128]{4,3,5,2,1,0:T(8,128)} %copy.120), kind=kLoop, calls=%fused_computation | loop fusion | flops 3145728 | bytes 12582912 | tf_op jit(solution)/shard_map/concatenate | solution.py:22
  246.8 3.1 fusion.116
  250.0 4.0 collective-permute-start.6
  254.0 1.6 copy.117
  255.6 1.6 copy.119
  257.3 5.5 %pad_maximum_fusion.2 = (f32[4,2,4,16,20,128]{5,4,3,2,1,0:T(8,128)}, f32[4,2,4,16,20,128]{5,4,3,2,1,0:T(8,128)}) fusion(f32[4,2,4,16,4,128]{5,4,3,2,1,0:T(4,128)S(1)} %copy.117, f32[4,1,4,16,16,128]{5,4,3,2,1,0:T(8,128)S(1)} %get-tuple-element.52, f32[4,1,4,16,16,128]{5,4,3,2,1,0:T(8,128)S(1)} %copy-done.2, f32[4,2,4,16,4,128]{5,4,3,2,1,0:T(4,128)S(1)} %copy.119), kind=kLoop, calls=%fused_computation.50 | loop fusion | flops 5242880 | bytes 16777216 | tf_op jit(solution)/shard_map/concatenate | solution.py:22
  262.7 22.1 %copy.123 = f32[4,2,4,16,24,128]{5,4,3,2,1,0:T(8,128)} copy(f32[4,2,4,16,24,128]{4,3,5,2,1,0:T(8,128)} %pad_maximum_fusion) | data formatting | bytes 12582912 | tf_op jit(solution)/shard_map/concatenate | solution.py:22
  284.8 6.1 %copy.125 = f32[4,2,4,16,24,4]{5,4,3,2,1,0:T(8,128)} copy(f32[4,2,4,16,24,4]{4,3,5,2,1,0:T(8,128)} %collective-permute-done.7) | data formatting | bytes 393216 | tf_op jit(solution)/shard_map/ppermute | solution.py:18
  290.9 7.1 %collective-permute-done.6 = f32[4,2,4,16,24,4]{4,3,5,2,1,0:T(8,128)} collective-permute-done((f32[4,2,4,16,24,4]{4,3,5,2,1,0:T(8,128)}, f32[4,2,4,16,24,4]{4,3,5,2,1,0:T(8,128)}, u32[]{:S(2)}, u32[]{:S(2)}) %collective-permute-start.6) | collective-permute-done | bytes 196640 | tf_op jit(solution)/shard_map/ppermute | solution.py:21
  298.0 6.0 %copy.124 = f32[4,2,4,16,24,4]{5,4,3,2,1,0:T(8,128)} copy(f32[4,2,4,16,24,4]{4,3,5,2,1,0:T(8,128)} %collective-permute-done.6) | data formatting | bytes 393216 | tf_op jit(solution)/shard_map/ppermute | solution.py:21
  304.1 63.1 %fusion.6 = f32[4,2,4,16,16,128]{5,4,3,2,1,0:T(8,128)} fusion(f32[4,2,4,16,24,4]{5,4,3,2,1,0:T(8,128)} %copy.125, f32[4,2,4,16,24,128]{5,4,3,2,1,0:T(8,128)} %copy.123, f32[4,2,4,16,24,4]{5,4,3,2,1,0:T(8,128)} %copy.124, f32[4,2,4,16,20,128]{5,4,3,2,1,0:T(8,128)} %get-tuple-element.47, f32[4,2,4,16,20,128]{5,4,3,2,1,0:T(8,128)} %get-tuple-element.46, ...), kind=kLoop, calls=%fused_computation.70 | loop fusion | flops 51380224 | bytes 82313216 | tf_op jit(solution)/shard_map/add | solution.py:46
  367.2 5.0 %subtract_reduce_fusion = (f32[4,4]{1,0:T(4,128)S(1)}, f32[4,4]{1,0:T(4,128)S(1)}, f32[4,4]{1,0:T(4,128)S(1)}, f32[4,4]{1,0:T(4,128)S(1)}) fusion(f32[4,2,4,16,16,128]{5,4,3,2,1,0:T(8,128)} %fusion.6, f32[4]{0:T(128)S(1)} %get-tuple-element.92, f32[4]{0:T(128)S(1)} %get-tuple-element.93, f32[4,16,16,128]{3,2,1,0:T(8,128)S(1)} %copy-done.8, ...), kind=kLoop, calls=%fused_computation.129 | loop fusion | flops 20447168 | bytes 6291872 | tf_op jit(solution)/shard_map/reduce_sum | solution.py:63
  372.2 10.4 %all-reduce.1 = (f32[4,4]{1,0:T(4,128)S(1)}, f32[4,4]{1,0:T(4,128)S(1)}, f32[4,4]{1,0:T(4,128)S(1)}, f32[4,4]{1,0:T(4,128)S(1)}) all-reduce(f32[4,4]{1,0:T(4,128)S(1)} %get-tuple-element.8, f32[4,4]{1,0:T(4,128)S(1)} %get-tuple-element.6, f32[4,4]{1,0:T(4,128)S(1)} %get-tuple-element.7, ...), channel_id=1, replica_groups=mesh['quad'=2,'py'=4,'pz'=4] {'pz'}, use_global_device_ids=true, to_apply=%region_9.10 | all-reduce | flops 64 | bytes 512 | tf_op jit(solution)/shard_map/psum | solution.py:119
  382.6 6.1 %all-reduce.2 = (f32[4,4]{1,0:T(4,128)S(1)}, f32[4,4]{1,0:T(4,128)S(1)}, f32[4,4]{1,0:T(4,128)S(1)}, f32[4,4]{1,0:T(4,128)S(1)}) all-reduce(f32[4,4]{1,0:T(4,128)S(1)} %get-tuple-element.17, f32[4,4]{1,0:T(4,128)S(1)} %get-tuple-element.18, f32[4,4]{1,0:T(4,128)S(1)} %get-tuple-element.19, ...), channel_id=1, replica_groups=mesh['quad'=2,'py'=4,'pz'=4] {'py'}, use_global_device_ids=true, to_apply=%region_10.11 | all-reduce | flops 64 | bytes 512 | tf_op jit(solution)/shard_map/psum | solution.py:119
  388.9 2.9 subtract_add_fusion
  391.8 4.4 fusion.34
  396.2 4.4 fusion.36
  400.6 4.6 add_bitcast_fusion
  405.2 4.9 %subtract_bitcast_fusion = f32[4,1,4,16,16,128]{5,0,4,3,2,1:T(4,128)S(1)} fusion(f32[4,4,16,16,128]{4,0,3,2,1:T(4,128)S(1)} %fusion.36, f32[4,4,16,16,128]{4,3,2,1,0:T(8,128)S(1)} %get-tuple-element.50, f32[4]{0:T(128)S(1)} %copy-done.20, f32[4]{0:T(128)S(1)} %copy-done.21, f32[]{:T(128)S(6)} %div.49), kind=kOutput, calls=%fused_computation.123 | convolution fusion | flops 25690144 | bytes 6291492 | tf_op jit(solution)/shard_map/kq,qsxyz->ksxyz/dot_general | solution.py:76
  410.1 2.0 pad_maximum_fusion.5
  412.2 2.6 copy.132
  414.8 51.8 %reduce-scatter.2.cloned.1.call-done = f32[4,2,4,8,16,128]{5,4,2,1,0,3:T(8,128)} async-done(((f32[4,2,4,16,16,128]{5,4,2,1,0,3:T(8,128)}), f32[4,2,4,8,16,128]{5,4,2,1,0,3:T(8,128)}) %reduce-scatter.2.cloned.1.call-update) | async-done | bytes 2097168 | tf_op jit(solution)/shard_map/reduce_scatter | solution.py:132
  466.6 3.2 copy.133
  (113 shorter events, 31.1 us)
Async XLA Ops:
  6.5 460.1 %reduce-scatter.2.cloned.1.call-start = ((), (), s32[]{:S(2)}) async-start(), calls=%async_computation.1 | async-start | bytes 6291456 | tf_op jit(solution)/shard_map/reduce_scatter | solution.py:132
  9.0 28.6 %collective-permute-start = (f32[1,2,4,16,4,128]{5,3,4,2,1,0:T(8,128)}, f32[1,2,4,16,4,128]{5,3,4,2,1,0:T(8,128)}, u32[]{:S(2)}, u32[]{:S(2)}) collective-permute-start(f32[1,2,4,16,4,128]{5,3,4,2,1,0:T(8,128)} %get-tuple-element.87), channel_id=1, source_target_pairs={{4,0},{8,4},{12,8},{0,12},{5,1},{9,5},{13,9},{1,13},{6,2},{10,6},{... | collective-permute-start | bytes 786440 | tf_op jit(solution)/shard_map/ppermute | solution.py:21
  11.4 26.2 %collective-permute-start.1 = (f32[1,2,4,16,4,128]{5,3,4,2,1,0:T(8,128)}, f32[1,2,4,16,4,128]{5,3,4,2,1,0:T(8,128)}, u32[]{:S(2)}, u32[]{:S(2)}) collective-permute-start(f32[1,2,4,16,4,128]{5,3,4,2,1,0:T(8,128)} %get-tuple-element.86), channel_id=1, source_target_pairs={{0,4},{4,8},{8,12},{12,0},{1,5},{5,9},{9,13},{13,1},{2,6},{6,10},{... | collective-permute-start | bytes 786440 | tf_op jit(solution)/shard_map/ppermute | solution.py:18
  20.0 6.3 %copy-start.14 = (f32[1,2,4,14,16,128]{5,3,4,2,1,0:T(8,128)S(1)}, f32[1,2,4,14,16,128]{5,3,4,2,1,0:T(8,128)}, u32[]{:S(2)}) copy-start(f32[1,2,4,14,16,128]{5,3,4,2,1,0:T(8,128)} %get-tuple-element.79) | copy-start | bytes 2752516
  20.0 7.5 %copy-start.19 = (f32[1,2,4,2,16,128]{5,3,4,2,1,0:T(2,128)S(1)}, f32[1,2,4,2,16,128]{5,3,4,2,1,0:T(2,128)}, u32[]{:S(2)}) copy-start(f32[1,2,4,2,16,128]{5,3,4,2,1,0:T(2,128)} %get-tuple-element.81) | copy-start | bytes 393220
  21.1 7.7 %copy-start.13 = (f32[1,2,4,14,16,128]{5,3,4,2,1,0:T(8,128)S(1)}, f32[1,2,4,14,16,128]{5,3,4,2,1,0:T(8,128)}, u32[]{:S(2)}) copy-start(f32[1,2,4,14,16,128]{5,3,4,2,1,0:T(8,128)} %get-tuple-element.78) | copy-start | bytes 2752516
  23.7 6.4 %copy-start.12 = (f32[1,2,4,13,16,128]{5,3,4,2,1,0:T(8,128)S(1)}, f32[1,2,4,13,16,128]{5,3,4,2,1,0:T(8,128)}, u32[]{:S(2)}) copy-start(f32[1,2,4,13,16,128]{5,3,4,2,1,0:T(8,128)} %get-tuple-element.75) | copy-start | bytes 2555908
  26.3 5.0 %copy-start.15 = (f32[1,2,4,3,16,128]{5,3,4,2,1,0:T(4,128)S(1)}, f32[1,2,4,3,16,128]{5,3,4,2,1,0:T(4,128)}, u32[]{:S(2)}) copy-start(f32[1,2,4,3,16,128]{5,3,4,2,1,0:T(4,128)} %get-tuple-element.77) | copy-start | bytes 589828
  27.5 5.1 %copy-start.11 = (f32[1,2,4,13,16,128]{5,3,4,2,1,0:T(8,128)S(1)}, f32[1,2,4,13,16,128]{5,3,4,2,1,0:T(8,128)}, u32[]{:S(2)}) copy-start(f32[1,2,4,13,16,128]{5,3,4,2,1,0:T(8,128)} %get-tuple-element.74) | copy-start | bytes 2555908
  30.1 4.9 %copy-start.17 = (f32[1,2,4,4,16,128]{5,3,4,2,1,0:T(4,128)S(1)}, f32[1,2,4,4,16,128]{5,3,4,2,1,0:T(4,128)}, u32[]{:S(2)}) copy-start(f32[1,2,4,4,16,128]{5,3,4,2,1,0:T(4,128)} %get-tuple-element.73) | copy-start | bytes 786436
  30.1 4.9 %copy-start.16 = (f32[1,2,4,4,16,128]{5,3,4,2,1,0:T(4,128)S(1)}, f32[1,2,4,4,16,128]{5,3,4,2,1,0:T(4,128)}, u32[]{:S(2)}) copy-start(f32[1,2,4,4,16,128]{5,3,4,2,1,0:T(4,128)} %get-tuple-element.72) | copy-start | bytes 786436
  44.0 13.5 %collective-permute-start.3 = (f32[1,2,4,16,24,4]{4,3,5,2,1,0:T(8,128)}, f32[1,2,4,16,24,4]{4,3,5,2,1,0:T(8,128)}, u32[]{:S(2)}, u32[]{:S(2)}) collective-permute-start(f32[1,2,4,16,24,4]{4,3,5,2,1,0:T(8,128)} %copy.95), channel_id=1, source_target_pairs={{0,1},{1,2},{2,3},{3,0},{4,5},{5,6},{6,7},{7,4},{8,9},{9,10},{10,1... | collective-permute-start | bytes 147464 | tf_op jit(solution)/shard_map/ppermute | solution.py:18
  48.5 12.1 %collective-permute-start.2 = (f32[1,2,4,16,24,4]{4,3,5,2,1,0:T(8,128)}, f32[1,2,4,16,24,4]{4,3,5,2,1,0:T(8,128)}, u32[]{:S(2)}, u32[]{:S(2)}) collective-permute-start(f32[1,2,4,16,24,4]{4,3,5,2,1,0:T(8,128)} %copy.92), channel_id=1, source_target_pairs={{1,0},{2,1},{3,2},{0,3},{5,4},{6,5},{7,6},{4,7},{9,8},{10,9},{11,1... | collective-permute-start | bytes 147464 | tf_op jit(solution)/shard_map/ppermute | solution.py:21
  55.8 7.8 %copy-start.3 = (f32[4,16,16,128]{3,2,1,0:T(8,128)S(1)}, f32[4,16,16,128]{3,2,1,0:T(8,128)}, u32[]{:S(2)}) copy-start(f32[4,16,16,128]{3,2,1,0:T(8,128)} %param.6) | copy-start | bytes 1572868
  55.8 7.8 %copy-start.4 = (f32[4,16,16,128]{3,2,1,0:T(8,128)S(1)}, f32[4,16,16,128]{3,2,1,0:T(8,128)}, u32[]{:S(2)}) copy-start(f32[4,16,16,128]{3,2,1,0:T(8,128)} %param.5) | copy-start | bytes 1572868
  55.8 7.8 %copy-start.18 = (f32[16,16,128]{2,1,0:T(8,128)S(1)}, f32[16,16,128]{2,1,0:T(8,128)}, u32[]{:S(2)}) copy-start(f32[16,16,128]{2,1,0:T(8,128)} %param.7) | copy-start | bytes 393220
  57.5 6.1 %copy-start.10 = (f32[1,2,4,16,16,128]{5,3,4,2,1,0:T(8,128)S(1)}, f32[1,2,4,16,16,128]{5,3,4,2,1,0:T(8,128)}, u32[]{:S(2)}) copy-start(f32[1,2,4,16,16,128]{5,3,4,2,1,0:T(8,128)} %get-tuple-element.56) | copy-start | bytes 3145732
  81.4 36.4 %copy-start.5 = (f32[4,16,16,128]{3,2,1,0:T(8,128)S(1)}, f32[4,16,16,128]{3,2,1,0:T(8,128)}, u32[]{:S(2)}) copy-start(f32[4,16,16,128]{3,2,1,0:T(8,128)} %param.5) | copy-start | bytes 1572868
  117.7 2.5 copy-start.22
  117.7 2.6 copy-start.24
  117.7 11.9 %copy-start.26 = (f32[4]{0:T(128)}, f32[4]{0:T(128)S(1)}, u32[]{:S(2)}) copy-start(f32[4]{0:T(128)S(1)} %get-tuple-element.15) | copy-start | bytes 52
  117.7 11.8 %copy-start.28 = (f32[4]{0:T(128)}, f32[4]{0:T(128)S(1)}, u32[]{:S(2)}) copy-start(f32[4]{0:T(128)S(1)} %get-tuple-element.16) | copy-start | bytes 52
  120.3 12.7 %copy-start = (f32[4,1,4,16,16,128]{5,4,3,2,1,0:T(8,128)}, f32[4,1,4,16,16,128]{5,4,3,2,1,0:T(8,128)S(1)}, u32[]{:S(2)}) copy-start(f32[4,1,4,16,16,128]{5,4,3,2,1,0:T(8,128)S(1)} %get-tuple-element.53) | copy-start | bytes 6291460
  131.2 34.3 %collective-permute-start.4 = (f32[4,2,4,16,4,128]{5,3,4,2,1,0:T(8,128)}, f32[4,2,4,16,4,128]{5,3,4,2,1,0:T(8,128)}, u32[]{:S(2)}, u32[]{:S(2)}) collective-permute-start(f32[4,2,4,16,4,128]{5,3,4,2,1,0:T(8,128)} %copy.144), channel_id=1, source_target_pairs={{4,0},{8,4},{12,8},{0,12},{5,1},{9,5},{13,9},{1,13},{6,2},{10,6},{... | collective-permute-start | bytes 3145736 | tf_op jit(solution)/shard_map/ppermute | solution.py:21
  132.3 52.1 %collective-permute-start.5 = (f32[4,2,4,16,4,128]{5,3,4,2,1,0:T(8,128)}, f32[4,2,4,16,4,128]{5,3,4,2,1,0:T(8,128)}, u32[]{:S(2)}, u32[]{:S(2)}) collective-permute-start(f32[4,2,4,16,4,128]{5,3,4,2,1,0:T(8,128)} %copy.145), channel_id=1, source_target_pairs={{0,4},{4,8},{8,12},{12,0},{1,5},{5,9},{9,13},{13,1},{2,6},{6,10},{... | collective-permute-start | bytes 3145736 | tf_op jit(solution)/shard_map/ppermute | solution.py:18
  152.8 2.6 copy-start.1
  249.9 7.3 %copy-start.2 = (f32[4,1,4,16,16,128]{5,4,3,2,1,0:T(8,128)S(1)}, f32[4,1,4,16,16,128]{5,4,3,2,1,0:T(8,128)}, u32[]{:S(2)}) copy-start(f32[4,1,4,16,16,128]{5,4,3,2,1,0:T(8,128)} %copy-done) | copy-start | bytes 6291460
  250.0 34.9 %collective-permute-start.7 = (f32[4,2,4,16,24,4]{4,3,5,2,1,0:T(8,128)}, f32[4,2,4,16,24,4]{4,3,5,2,1,0:T(8,128)}, u32[]{:S(2)}, u32[]{:S(2)}) collective-permute-start(f32[4,2,4,16,24,4]{4,3,5,2,1,0:T(8,128)} %get-tuple-element.29), channel_id=1, source_target_pairs={{0,1},{1,2},{2,3},{3,0},{4,5},{5,6},{6,7},{7,4},{8,9},{9,10},{10,1... | collective-permute-start | bytes 589832 | tf_op jit(solution)/shard_map/ppermute | solution.py:18
  250.0 48.1 %collective-permute-start.6 = (f32[4,2,4,16,24,4]{4,3,5,2,1,0:T(8,128)}, f32[4,2,4,16,24,4]{4,3,5,2,1,0:T(8,128)}, u32[]{:S(2)}, u32[]{:S(2)}) collective-permute-start(f32[4,2,4,16,24,4]{4,3,5,2,1,0:T(8,128)} %get-tuple-element.28), channel_id=1, source_target_pairs={{1,0},{2,1},{3,2},{0,3},{5,4},{6,5},{7,6},{4,7},{9,8},{10,9},{11,1... | collective-permute-start | bytes 589832 | tf_op jit(solution)/shard_map/ppermute | solution.py:21
  304.1 63.1 %copy-start.6 = (f32[4,16,16,128]{3,2,1,0:T(8,128)S(1)}, f32[4,16,16,128]{3,2,1,0:T(8,128)}, u32[]{:S(2)}) copy-start(f32[4,16,16,128]{3,2,1,0:T(8,128)} %get-tuple-element.64) | copy-start | bytes 1572868
  304.1 63.1 %copy-start.8 = (f32[4,16,16,128]{3,2,1,0:T(8,128)S(1)}, f32[4,16,16,128]{3,2,1,0:T(8,128)}, u32[]{:S(2)}) copy-start(f32[4,16,16,128]{3,2,1,0:T(8,128)} %get-tuple-element.65) | copy-start | bytes 1572868
  367.1 21.5 %copy-start.23 = (f32[4]{0:T(128)S(1)}, f32[4]{0:T(128)}, u32[]{:S(2)}) copy-start(f32[4]{0:T(128)} %copy-done.22) | copy-start | bytes 52
  367.2 21.5 %copy-start.25 = (f32[4]{0:T(128)S(1)}, f32[4]{0:T(128)}, u32[]{:S(2)}) copy-start(f32[4]{0:T(128)} %copy-done.24) | copy-start | bytes 52
  367.2 21.5 %copy-start.27 = (f32[4]{0:T(128)S(1)}, f32[4]{0:T(128)}, u32[]{:S(2)}) copy-start(f32[4]{0:T(128)} %copy-done.26) | copy-start | bytes 52
  367.2 21.5 %copy-start.29 = (f32[4]{0:T(128)S(1)}, f32[4]{0:T(128)}, u32[]{:S(2)}) copy-start(f32[4]{0:T(128)} %copy-done.28) | copy-start | bytes 52
  367.2 21.5 %copy-start.30 = (f32[4]{0:T(128)S(1)}, f32[4]{0:T(128)}, u32[]{:S(2)}) copy-start(f32[4]{0:T(128)} %multiply_add_fusion.4) | copy-start | bytes 52
  367.2 21.6 %copy-start.7 = (f32[4,16,16,128]{3,2,1,0:T(8,128)S(1)}, f32[4,16,16,128]{3,2,1,0:T(8,128)}, u32[]{:S(2)}) copy-start(f32[4,16,16,128]{3,2,1,0:T(8,128)} %get-tuple-element.64) | copy-start | bytes 1572868
  367.2 21.6 %copy-start.9 = (f32[4,16,16,128]{3,2,1,0:T(8,128)S(1)}, f32[4,16,16,128]{3,2,1,0:T(8,128)}, u32[]{:S(2)}) copy-start(f32[4,16,16,128]{3,2,1,0:T(8,128)} %get-tuple-element.65) | copy-start | bytes 1572868
  388.9 2.9 copy-start.20
  388.9 2.9 copy-start.21
Sparse Core Ops, SparseCore 0:
  414.9 51.6 reduce-scatter.1
